TPU v7x, 32 devices: a whole 2x2x4 slice. The times are simulated.
32 devices in a mesh: ty: 4 (over y, x), tx: 4 (over z), corner: 2 (over core).
Axes of the slice: x: 2, y: 2, z: 4, core: 2. Of those that a mesh axis runs over, the one named last changes fastest.
Arguments:
- level_init: int32 [1024, 1024], P('ty', 'tx'), may hold values from -64 to 64
- target: int32 [1024, 1024], P('ty', 'tx'), may hold values 0 or 1
- kernels: float32 [2, 5, 2, 128, 128], P('corner'), may hold values from -12 to 12
- corner_doses: float32 [2], P('corner'), may hold values from 0.7 to 1.4
Outputs:
- resist: float32 [2, 1024, 1024], P('corner', 'ty', 'tx')
- level_set: float32 [1024, 1024], P('ty', 'tx')
All inputs are finite; a program needn't handle non-finite values. No bound on the sum of `target` on one device may be relied on, other than what follows from the above.
Results may differ from a plain program's by a relative error of at most 0.015.
The roundings to bfloat16 on the way count: a program that leaves them out, or rounds other values in their place, can miss the bound.
Values may be sent and summed in bfloat16 or wider, within the bound.
No kernel may reach another device: no remote copies, remote signals or barrier semaphores. Data moves between devices by JAX's collectives and lax.ppermute only.
A program may use at most 64 MiB of HBM per device.

v0:
```python
import math
import jax
import jax.numpy as jnp
from jax import lax
from jax.sharding import PartitionSpec as P

HALO = 128
KF = 128
LS_STEPS = 3
STEEPNESS = 4.0
THRESHOLD = 1.0
SPEED_GAIN = 4.0
SMOOTHING = 0.24
GRAD_FLOOR = 0.25


def with_halo(block, sides, width):
    for axis, dim in sides:
        count = lax.axis_size(axis)
        forward = [(i, i + 1) for i in range(count - 1)]
        backward = [(target, source) for source, target in forward]
        low = lax.ppermute(
            lax.slice_in_dim(block, block.shape[dim] - width, None, axis=dim), axis, forward
        )
        high = lax.ppermute(lax.slice_in_dim(block, 0, width, axis=dim), axis, backward)
        block = jnp.concatenate([low, block, high], axis=dim)
    return block


def make_tables(window, freqs, margin, tile):
    shifts = jnp.arange(freqs, dtype=jnp.int32) - freqs // 2
    places = jnp.arange(window, dtype=jnp.int32)
    phases = shifts[:, None] * places[None, :] % window
    angles = 2.0 * math.pi / window * phases.astype(jnp.float32)
    scaled = 1.0 / math.sqrt(window)
    fwd_cos = (jnp.cos(angles) * scaled).astype(jnp.bfloat16)
    fwd_sin = (-jnp.sin(angles) * scaled).astype(jnp.bfloat16)
    inner = angles[:, margin : margin + tile].T
    inv_cos = (jnp.cos(inner) * scaled).astype(jnp.bfloat16)
    inv_sin = (jnp.sin(inner) * scaled).astype(jnp.bfloat16)
    return (fwd_cos, fwd_sin, inv_cos, inv_sin)


def matmul(left, right):
    return jnp.dot(left, right, preferred_element_type=jnp.float32)


def batched(form, left, right):
    return jnp.einsum(form, left, right, preferred_element_type=jnp.float32)


def tile_pass(win_data, goal, kernel_re, kernel_im, doses_col, tables):
    fwd_cos, fwd_sin, inv_cos, inv_sin = tables
    freqs = fwd_cos.shape[0]
    lift = matmul(jnp.concatenate([fwd_cos, fwd_sin], axis=0), win_data).astype(jnp.bfloat16)
    lift_re = lift[:freqs]
    lift_im = lift[freqs:]
    spec_re = matmul(lift_re, fwd_cos.T) - matmul(lift_im, fwd_sin.T)
    spec_im = matmul(lift_re, fwd_sin.T) + matmul(lift_im, fwd_cos.T)
    blur_re = (kernel_re * spec_re - kernel_im * spec_im).astype(jnp.bfloat16)
    blur_im = (kernel_re * spec_im + kernel_im * spec_re).astype(jnp.bfloat16)
    proj_re = (
        batched("rj,gjk->grk", inv_cos, blur_re) - batched("rj,gjk->grk", inv_sin, blur_im)
    ).astype(jnp.bfloat16)
    proj_im = (
        batched("rj,gjk->grk", inv_cos, blur_im) + batched("rj,gjk->grk", inv_sin, blur_re)
    ).astype(jnp.bfloat16)
    field_re = batched("grj,cj->grc", proj_re, inv_cos) - batched("grj,cj->grc", proj_im, inv_sin)
    field_im = batched("grj,cj->grc", proj_re, inv_sin) + batched("grj,cj->grc", proj_im, inv_cos)
    groups = doses_col.shape[0]
    tile = field_re.shape[1]
    grouped = (groups, -1, tile, tile)
    power = (field_re * field_re + field_im * field_im).reshape(grouped)
    intensity = jnp.sum(power, axis=1)
    dose_col = doses_col[:, None, None]
    resist = jax.nn.sigmoid(STEEPNESS * (dose_col * intensity - THRESHOLD))
    sens = 2.0 * (resist - goal) * STEEPNESS * dose_col * resist * (1.0 - resist)
    adj_re = (
        (2.0 * sens[:, None] * field_re.reshape(grouped))
        .reshape(field_re.shape)
        .astype(jnp.bfloat16)
    )
    adj_im = (
        (2.0 * sens[:, None] * field_im.reshape(grouped))
        .reshape(field_im.shape)
        .astype(jnp.bfloat16)
    )
    back_re = (
        batched("grc,cj->grj", adj_re, inv_cos) + batched("grc,cj->grj", adj_im, inv_sin)
    ).astype(jnp.bfloat16)
    back_im = (
        batched("grc,cj->grj", adj_im, inv_cos) - batched("grc,cj->grj", adj_re, inv_sin)
    ).astype(jnp.bfloat16)
    grad_blur_re = batched("rj,grk->gjk", inv_cos, back_re) + batched(
        "rj,grk->gjk", inv_sin, back_im
    )
    grad_blur_im = batched("rj,grk->gjk", inv_cos, back_im) - batched(
        "rj,grk->gjk", inv_sin, back_re
    )
    grad_spec_re = jnp.sum(kernel_re * grad_blur_re + kernel_im * grad_blur_im, axis=0)
    grad_spec_im = jnp.sum(kernel_re * grad_blur_im - kernel_im * grad_blur_re, axis=0)
    return (resist, grad_spec_re, grad_spec_im)


def window_grad(grad_spec_re, grad_spec_im, tables):
    fwd_cos, fwd_sin = (tables[0], tables[1])
    spec_low_re = grad_spec_re.astype(jnp.bfloat16)
    spec_low_im = grad_spec_im.astype(jnp.bfloat16)
    grad_lift_re = (matmul(spec_low_re, fwd_cos) + matmul(spec_low_im, fwd_sin)).astype(
        jnp.bfloat16
    )
    grad_lift_im = (matmul(spec_low_im, fwd_cos) - matmul(spec_low_re, fwd_sin)).astype(
        jnp.bfloat16
    )
    stacked = jnp.concatenate([fwd_cos, fwd_sin], axis=0)
    grad_lift = jnp.concatenate([grad_lift_re, grad_lift_im], axis=0)
    result = lax.dot_general(
        stacked, grad_lift, (((0,), (0,)), ((), ())), preferred_element_type=jnp.float32
    )
    return result.astype(jnp.bfloat16)


def fold_axis(values, tile, margin, axis):
    centre = lax.slice_in_dim(values, 2 * margin, 2 * margin + tile, axis=axis)
    upper_rim = lax.slice_in_dim(values, 0, margin, axis=axis)
    lower_rim = lax.slice_in_dim(values, tile + 3 * margin, tile + 4 * margin, axis=axis)
    leading = [(0, 0), (0, 0)]
    trailing = [(0, 0), (0, 0)]
    leading[axis] = (0, tile - margin)
    trailing[axis] = (tile - margin, 0)
    return centre + jnp.pad(upper_rim, leading) + jnp.pad(lower_rim, trailing)


def advance(padded, speed):
    centre = padded[1:-1, 1:-1]
    above_cells = padded[:-2, 1:-1]
    below_cells = padded[2:, 1:-1]
    left_cells = padded[1:-1, :-2]
    right_cells = padded[1:-1, 2:]
    slope_y = 0.5 * (below_cells - above_cells)
    slope_x = 0.5 * (right_cells - left_cells)
    spread = above_cells + below_cells + left_cells + right_cells - 4.0 * centre
    return (
        centre
        - SPEED_GAIN * speed * jnp.sqrt(GRAD_FLOOR + slope_y * slope_y + slope_x * slope_x)
        + SMOOTHING * spread
    )


def body(level_init, target, kernels, corner_doses):
    tile = level_init.shape[0]
    margin = HALO
    freqs = KF
    window = tile + 2 * margin
    tables = make_tables(window, freqs, margin, tile)
    level = level_init.astype(jnp.float32) * 0.125
    trans = jnp.tanh(0.25 * level)
    level_rim = with_halo(level.astype(jnp.bfloat16), (("ty", 0), ("tx", 1)), margin).astype(
        level.dtype
    )
    win_data = jnp.tanh(0.25 * level_rim).astype(jnp.bfloat16)
    kernel_re = kernels[:, :, 0].reshape(-1, freqs, freqs)
    kernel_im = kernels[:, :, 1].reshape(-1, freqs, freqs)
    resist, grad_spec_re, grad_spec_im = tile_pass(
        win_data, target.astype(jnp.float32), kernel_re, kernel_im, corner_doses, tables
    )
    grad_spec_re, grad_spec_im = (
        lax.psum(grad_spec_re.astype(jnp.bfloat16), "corner").astype(jnp.float32),
        lax.psum(grad_spec_im.astype(jnp.bfloat16), "corner").astype(jnp.float32),
    )
    grad_window = window_grad(grad_spec_re, grad_spec_im, tables)
    framed_grad = with_halo(grad_window, (("ty", 0), ("tx", 1)), margin).astype(jnp.float32)
    grad_trans = fold_axis(fold_axis(framed_grad, tile, margin, 0), tile, margin, 1)
    speed = grad_trans * 0.25 * (1.0 - trans * trans)
    stacked = jnp.stack([level, speed], axis=1)
    grown = with_halo(stacked.astype(jnp.bfloat16), (("ty", 0), ("tx", 2)), LS_STEPS).astype(
        stacked.dtype
    )
    level_ext = grown[:, 0, :]
    speed_ext = grown[:, 1, :]
    extent = tile + 2 * LS_STEPS
    offsets = jnp.arange(extent, dtype=jnp.int32) - LS_STEPS
    rows_at = lax.axis_index("ty") * tile + offsets
    cols_at = lax.axis_index("tx") * tile + offsets
    inside_rows = (rows_at >= 0) & (rows_at < tile * lax.axis_size("ty"))
    inside_cols = (cols_at >= 0) & (cols_at < tile * lax.axis_size("tx"))
    inside = (inside_rows[:, None] & inside_cols[None, :]).astype(jnp.float32)
    for repeat in range(LS_STEPS):
        speed_ext = speed_ext[1:-1, 1:-1]
        level_ext = (
            advance(level_ext, speed_ext)
            * inside[repeat + 1 : extent - repeat - 1, repeat + 1 : extent - repeat - 1]
        )
    level = level_ext
    return (resist, level)


def solution(mesh):
    in_specs = (P("ty", "tx"), P("ty", "tx"), P("corner", None, None, None, None), P("corner"))
    out_specs = (P("corner", "ty", "tx"), P("ty", "tx"))
    return jax.shard_map(body, mesh=mesh, in_specs=in_specs, out_specs=out_specs, check_vma=False)
```

profile of v0, /device:TPU:0, one launch (start us, length us, event | category | flops | bytes accessed | tf_op | source)
XLA Modules:
  0.0 120.3 jit_solution(7993260280615964932)
XLA Ops:
  8.2 4.9 %collective-permute-start = (bf16[128,256]{1,0:T(8,128)(2,1)S(1)}, bf16[128,256]{1,0:T(8,128)(2,1)S(1)}, u32[]{:S(2)}, u32[]{:S(2)}) collective-permute-start(bf16[128,256]{1,0:T(8,128)(2,1)S(1)} %get-tuple-element.26), channel_id=1, source_target_pairs={{0,8},{8,16},{16,24},{1,9},{9,17},{17,25},{2,10},{10,18},{18,26},{... | collective-permute-start | bytes 196616 | tf_op jit(solution)/shard_map/ppermute | solution.py:22
  13.1 1.3 %collective-permute-start.1 = (bf16[128,256]{1,0:T(8,128)(2,1)S(1)}, bf16[128,256]{1,0:T(8,128)(2,1)S(1)}, u32[]{:S(2)}, u32[]{:S(2)}) collective-permute-start(bf16[128,256]{1,0:T(8,128)(2,1)S(1)} %get-tuple-element.27), channel_id=1, source_target_pairs={{8,0},{16,8},{24,16},{9,1},{17,9},{25,17},{10,2},{18,10},{26,18},{... | collective-permute-start | bytes 196616 | tf_op jit(solution)/shard_map/ppermute | solution.py:25
  14.4 1.1 fusion.118
  15.5 1.1 fusion.38
  17.7 1.6 %collective-permute-done.1 = bf16[128,256]{1,0:T(8,128)(2,1)S(1)} collective-permute-done((bf16[128,256]{1,0:T(8,128)(2,1)S(1)}, bf16[128,256]{1,0:T(8,128)(2,1)S(1)}, u32[]{:S(2)}, u32[]{:S(2)}) %collective-permute-start.1) | collective-permute-done | bytes 65568 | tf_op jit(solution)/shard_map/ppermute | solution.py:25
  19.3 3.5 %collective-permute-start.2 = (bf16[512,128]{1,0:T(8,128)(2,1)S(1)}, bf16[512,128]{1,0:T(8,128)(2,1)S(1)}, u32[]{:S(2)}, u32[]{:S(2)}) collective-permute-start(bf16[512,128]{1,0:T(8,128)(2,1)S(1)} %get-tuple-element.24), channel_id=1, source_target_pairs={{0,2},{2,4},{4,6},{1,3},{3,5},{5,7},{8,10},{10,12},{12,14},{9,11},... | collective-permute-start | bytes 393224 | tf_op jit(solution)/shard_map/ppermute | solution.py:22
  22.8 1.3 %collective-permute-start.3 = (bf16[512,128]{1,0:T(8,128)(2,1)S(1)}, bf16[512,128]{1,0:T(8,128)(2,1)S(1)}, u32[]{:S(2)}, u32[]{:S(2)}) collective-permute-start(bf16[512,128]{1,0:T(8,128)(2,1)S(1)} %get-tuple-element.25), channel_id=1, source_target_pairs={{2,0},{4,2},{6,4},{3,1},{5,3},{7,5},{10,8},{12,10},{14,12},{11,9},... | collective-permute-start | bytes 393224 | tf_op jit(solution)/shard_map/ppermute | solution.py:25
  25.3 4.4 %collective-permute-done.3 = bf16[512,128]{1,0:T(8,128)(2,1)S(1)} collective-permute-done((bf16[512,128]{1,0:T(8,128)(2,1)S(1)}, bf16[512,128]{1,0:T(8,128)(2,1)S(1)}, u32[]{:S(2)}, u32[]{:S(2)}) %collective-permute-start.3) | collective-permute-done | bytes 131104 | tf_op jit(solution)/shard_map/ppermute | solution.py:25
  30.0 1.2 fusion.55
  31.2 1.2 %fusion.56 = f32[128,128]{1,0:T(8,128)S(1)} fusion(s32[128]{0:T(128)S(1)} %iota_add_fusion.1, bf16[256,512]{1,0:T(8,128)(2,1)S(1)} %convolution_convert_fusion.1), kind=kOutput, calls=%fused_computation.112 | convolution fusion | flops 17891328 | bytes 197120 | tf_op jit(solution)/shard_map/dot_general | solution.py:45
  32.4 1.2 %convolution_subtract_fusion.5 = f32[128,128]{1,0:T(8,128)S(1)} fusion(f32[128,128]{1,0:T(8,128)S(1)} %fusion.55, s32[128]{0:T(128)S(1)} %iota_add_fusion.1, bf16[256,512]{1,0:T(8,128)(2,1)S(1)} %convolution_convert_fusion.1), kind=kOutput, calls=%fused_computation.27 | convolution fusion | flops 17907712 | bytes 262656 | tf_op jit(solution)/shard_map/dot_general | solution.py:45
  33.7 1.2 convolution_add_fusion.5
  42.2 18.1 %all-reduce.5.cloned.1.call-done = (bf16[128,128]{0,1:T(8,128)(2,1)}, bf16[128,128]{0,1:T(8,128)(2,1)}) async-done(((bf16[128,128]{0,1:T(8,128)(2,1)}, bf16[128,128]{0,1:T(8,128)(2,1)}), (bf16[128,128]{0,1:T(8,128)(2,1)}, bf16[128,128]{0,1:T(8,128)(2,1)})) %all-reduce.5.cloned.1.call-update) | async-done | bytes 65552 | tf_op jit(solution)/shard_map/psum | solution.py:169
  60.3 2.0 %fusion.54 = f32[128,512]{1,0:T(8,128)S(1)} fusion(bf16[128,128]{0,1:T(8,128)(2,1)} %get-tuple-element.5, s32[128]{0:T(128)S(1)} %iota_add_fusion.1), kind=kOutput, calls=%fused_computation.110 | convolution fusion | flops 17825792 | bytes 295424 | tf_op jit(solution)/shard_map/dot_general | solution.py:45
  62.3 2.0 %fusion.53 = f32[128,512]{1,0:T(8,128)S(1)} fusion(bf16[128,128]{0,1:T(8,128)(2,1)} %get-tuple-element.4, s32[128]{0:T(128)S(1)} %iota_add_fusion.1), kind=kOutput, calls=%fused_computation.109 | convolution fusion | flops 17825792 | bytes 295424 | tf_op jit(solution)/shard_map/dot_general | solution.py:45
  64.3 1.4 %fusion.8 = bf16[128,512]{1,0:T(8,128)(2,1)S(1)} fusion(f32[128,512]{1,0:T(8,128)S(1)} %fusion.54, bf16[128,128]{0,1:T(8,128)(2,1)S(1)} %copy-done.4, s32[128]{0:T(128)S(1)} %iota_add_fusion.1), kind=kOutput, calls=%fused_computation.24 | convolution fusion | flops 18022400 | bytes 426496 | tf_op jit(solution)/shard_map/dot_general | solution.py:45
  65.7 1.2 fusion.9
  67.2 3.7 %collective-permute-start.4 = (bf16[128,512]{1,0:T(8,128)(2,1)S(1)}, bf16[128,512]{1,0:T(8,128)(2,1)S(1)}, u32[]{:S(2)}, u32[]{:S(2)}) collective-permute-start(bf16[128,512]{1,0:T(8,128)(2,1)S(1)} %get-tuple-element.14), channel_id=1, source_target_pairs={{0,8},{8,16},{16,24},{1,9},{9,17},{17,25},{2,10},{10,18},{18,26},{... | collective-permute-start | bytes 393224 | tf_op jit(solution)/shard_map/ppermute | solution.py:22
  70.9 1.3 %collective-permute-start.5 = (bf16[128,512]{1,0:T(8,128)(2,1)S(1)}, bf16[128,512]{1,0:T(8,128)(2,1)S(1)}, u32[]{:S(2)}, u32[]{:S(2)}) collective-permute-start(bf16[128,512]{1,0:T(8,128)(2,1)S(1)} %get-tuple-element.15), channel_id=1, source_target_pairs={{8,0},{16,8},{24,16},{9,1},{17,9},{25,17},{10,2},{18,10},{26,18},{... | collective-permute-start | bytes 393224 | tf_op jit(solution)/shard_map/ppermute | solution.py:25
  72.2 1.8 %collective-permute-done.4 = bf16[128,512]{1,0:T(8,128)(2,1)S(1)} collective-permute-done((bf16[128,512]{1,0:T(8,128)(2,1)S(1)}, bf16[128,512]{1,0:T(8,128)(2,1)S(1)}, u32[]{:S(2)}, u32[]{:S(2)}) %collective-permute-start.4) | collective-permute-done | bytes 131104 | tf_op jit(solution)/shard_map/ppermute | solution.py:22
  74.1 4.7 %collective-permute-done.5 = bf16[128,512]{1,0:T(8,128)(2,1)S(1)} collective-permute-done((bf16[128,512]{1,0:T(8,128)(2,1)S(1)}, bf16[128,512]{1,0:T(8,128)(2,1)S(1)}, u32[]{:S(2)}, u32[]{:S(2)}) %collective-permute-start.5) | collective-permute-done | bytes 131104 | tf_op jit(solution)/shard_map/ppermute | solution.py:25
  78.8 3.4 %collective-permute-start.6 = (bf16[768,128]{1,0:T(8,128)(2,1)S(1)}, bf16[768,128]{1,0:T(8,128)(2,1)S(1)}, u32[]{:S(2)}, u32[]{:S(2)}) collective-permute-start(bf16[768,128]{1,0:T(8,128)(2,1)S(1)} %get-tuple-element.8), channel_id=1, source_target_pairs={{0,2},{2,4},{4,6},{1,3},{3,5},{5,7},{8,10},{10,12},{12,14},{9,11},... | collective-permute-start | bytes 589832 | tf_op jit(solution)/shard_map/ppermute | solution.py:22
  82.2 1.3 %collective-permute-start.7 = (bf16[768,128]{1,0:T(8,128)(2,1)S(1)}, bf16[768,128]{1,0:T(8,128)(2,1)S(1)}, u32[]{:S(2)}, u32[]{:S(2)}) collective-permute-start(bf16[768,128]{1,0:T(8,128)(2,1)S(1)} %get-tuple-element.9), channel_id=1, source_target_pairs={{2,0},{4,2},{6,4},{3,1},{5,3},{7,5},{10,8},{12,10},{14,12},{11,9},... | collective-permute-start | bytes 589832 | tf_op jit(solution)/shard_map/ppermute | solution.py:25
  83.6 2.5 %collective-permute-done.6 = bf16[768,128]{1,0:T(8,128)(2,1)S(1)} collective-permute-done((bf16[768,128]{1,0:T(8,128)(2,1)S(1)}, bf16[768,128]{1,0:T(8,128)(2,1)S(1)}, u32[]{:S(2)}, u32[]{:S(2)}) %collective-permute-start.6) | collective-permute-done | bytes 196640 | tf_op jit(solution)/shard_map/ppermute | solution.py:22
  86.0 4.1 %collective-permute-done.7 = bf16[768,128]{1,0:T(8,128)(2,1)S(1)} collective-permute-done((bf16[768,128]{1,0:T(8,128)(2,1)S(1)}, bf16[768,128]{1,0:T(8,128)(2,1)S(1)}, u32[]{:S(2)}, u32[]{:S(2)}) %collective-permute-start.7) | collective-permute-done | bytes 196640 | tf_op jit(solution)/shard_map/ppermute | solution.py:25
  91.2 3.3 %collective-permute-start.8 = (bf16[3,2,256]{2,0,1:T(4,128)(2,1)S(1)}, bf16[3,2,256]{2,0,1:T(4,128)(2,1)S(1)}, u32[]{:S(2)}, u32[]{:S(2)}) collective-permute-start(bf16[3,2,256]{2,0,1:T(4,128)(2,1)S(1)} %get-tuple-element.18), channel_id=1, source_target_pairs={{0,8},{8,16},{16,24},{1,9},{9,17},{17,25},{2,10},{10,18},{18,26},{... | collective-permute-start | bytes 9224 | tf_op jit(solution)/shard_map/ppermute | solution.py:22
  94.5 1.3 %collective-permute-start.9 = (bf16[3,2,256]{2,0,1:T(4,128)(2,1)S(1)}, bf16[3,2,256]{2,0,1:T(4,128)(2,1)S(1)}, u32[]{:S(2)}, u32[]{:S(2)}) collective-permute-start(bf16[3,2,256]{2,0,1:T(4,128)(2,1)S(1)} %get-tuple-element.19), channel_id=1, source_target_pairs={{8,0},{16,8},{24,16},{9,1},{17,9},{25,17},{10,2},{18,10},{26,18},{... | collective-permute-start | bytes 9224 | tf_op jit(solution)/shard_map/ppermute | solution.py:25
  95.8 4.2 %collective-permute-done.9 = bf16[3,2,256]{2,0,1:T(4,128)(2,1)S(1)} collective-permute-done((bf16[3,2,256]{2,0,1:T(4,128)(2,1)S(1)}, bf16[3,2,256]{2,0,1:T(4,128)(2,1)S(1)}, u32[]{:S(2)}, u32[]{:S(2)}) %collective-permute-start.9) | collective-permute-done | bytes 3104 | tf_op jit(solution)/shard_map/ppermute | solution.py:25
  100.2 3.4 %collective-permute-start.10 = (bf16[262,2,3]{2,0,1:T(8,128)(2,1)S(1)}, bf16[262,2,3]{2,0,1:T(8,128)(2,1)S(1)}, u32[]{:S(2)}, u32[]{:S(2)}) collective-permute-start(bf16[262,2,3]{2,0,1:T(8,128)(2,1)S(1)} %get-tuple-element.16), channel_id=1, source_target_pairs={{0,2},{2,4},{4,6},{1,3},{3,5},{5,7},{8,10},{10,12},{12,14},{9,11},... | collective-permute-start | bytes 9440 | tf_op jit(solution)/shard_map/ppermute | solution.py:22
  103.6 1.3 %collective-permute-start.11 = (bf16[262,2,3]{2,0,1:T(8,128)(2,1)S(1)}, bf16[262,2,3]{2,0,1:T(8,128)(2,1)S(1)}, u32[]{:S(2)}, u32[]{:S(2)}) collective-permute-start(bf16[262,2,3]{2,0,1:T(8,128)(2,1)S(1)} %get-tuple-element.17), channel_id=1, source_target_pairs={{2,0},{4,2},{6,4},{3,1},{5,3},{7,5},{10,8},{12,10},{14,12},{11,9},... | collective-permute-start | bytes 9440 | tf_op jit(solution)/shard_map/ppermute | solution.py:25
  106.1 4.4 %collective-permute-done.11 = bf16[262,2,3]{2,0,1:T(8,128)(2,1)S(1)} collective-permute-done((bf16[262,2,3]{2,0,1:T(8,128)(2,1)S(1)}, bf16[262,2,3]{2,0,1:T(8,128)(2,1)S(1)}, u32[]{:S(2)}, u32[]{:S(2)}) %collective-permute-start.11) | collective-permute-done | bytes 3176 | tf_op jit(solution)/shard_map/ppermute | solution.py:25
  112.3 1.2 slice_multiply_fusion.4
  (63 shorter events, 14.7 us)
Async XLA Ops:
  7.2 53.2 %all-reduce.5.cloned.1.call-start = ((), (), s32[]{:S(2)}) async-start(), calls=%async_computation | async-start | bytes 131072 | tf_op jit(solution)/shard_map/psum | solution.py:169
  8.2 9.5 %collective-permute-start = (bf16[128,256]{1,0:T(8,128)(2,1)S(1)}, bf16[128,256]{1,0:T(8,128)(2,1)S(1)}, u32[]{:S(2)}, u32[]{:S(2)}) collective-permute-start(bf16[128,256]{1,0:T(8,128)(2,1)S(1)} %get-tuple-element.26), channel_id=1, source_target_pairs={{0,8},{8,16},{16,24},{1,9},{9,17},{17,25},{2,10},{10,18},{18,26},{... | collective-permute-start | bytes 196616 | tf_op jit(solution)/shard_map/ppermute | solution.py:22
  13.1 6.2 %collective-permute-start.1 = (bf16[128,256]{1,0:T(8,128)(2,1)S(1)}, bf16[128,256]{1,0:T(8,128)(2,1)S(1)}, u32[]{:S(2)}, u32[]{:S(2)}) collective-permute-start(bf16[128,256]{1,0:T(8,128)(2,1)S(1)} %get-tuple-element.27), channel_id=1, source_target_pairs={{8,0},{16,8},{24,16},{9,1},{17,9},{25,17},{10,2},{18,10},{26,18},{... | collective-permute-start | bytes 196616 | tf_op jit(solution)/shard_map/ppermute | solution.py:25
  19.3 6.0 %collective-permute-start.2 = (bf16[512,128]{1,0:T(8,128)(2,1)S(1)}, bf16[512,128]{1,0:T(8,128)(2,1)S(1)}, u32[]{:S(2)}, u32[]{:S(2)}) collective-permute-start(bf16[512,128]{1,0:T(8,128)(2,1)S(1)} %get-tuple-element.24), channel_id=1, source_target_pairs={{0,2},{2,4},{4,6},{1,3},{3,5},{5,7},{8,10},{10,12},{12,14},{9,11},... | collective-permute-start | bytes 393224 | tf_op jit(solution)/shard_map/ppermute | solution.py:22
  22.8 6.9 %collective-permute-start.3 = (bf16[512,128]{1,0:T(8,128)(2,1)S(1)}, bf16[512,128]{1,0:T(8,128)(2,1)S(1)}, u32[]{:S(2)}, u32[]{:S(2)}) collective-permute-start(bf16[512,128]{1,0:T(8,128)(2,1)S(1)} %get-tuple-element.25), channel_id=1, source_target_pairs={{2,0},{4,2},{6,4},{3,1},{5,3},{7,5},{10,8},{12,10},{14,12},{11,9},... | collective-permute-start | bytes 393224 | tf_op jit(solution)/shard_map/ppermute | solution.py:25
  37.1 1.0 copy-start.1
  60.3 3.9 %copy-start.4 = (bf16[128,128]{0,1:T(8,128)(2,1)S(1)}, bf16[128,128]{0,1:T(8,128)(2,1)}, u32[]{:S(2)}) copy-start(bf16[128,128]{0,1:T(8,128)(2,1)} %get-tuple-element.4) | copy-start | bytes 98308
  62.3 3.4 %copy-start.3 = (bf16[128,128]{0,1:T(8,128)(2,1)S(1)}, bf16[128,128]{0,1:T(8,128)(2,1)}, u32[]{:S(2)}) copy-start(bf16[128,128]{0,1:T(8,128)(2,1)} %get-tuple-element.5) | copy-start | bytes 98308
  66.9 16.7 %copy-start = (s32[256,256]{1,0:T(8,128)S(1)}, s32[256,256]{1,0:T(8,128)}, u32[]{:S(2)}) copy-start(s32[256,256]{1,0:T(8,128)} %param.4) | copy-start | bytes 786436
  67.2 6.8 %collective-permute-start.4 = (bf16[128,512]{1,0:T(8,128)(2,1)S(1)}, bf16[128,512]{1,0:T(8,128)(2,1)S(1)}, u32[]{:S(2)}, u32[]{:S(2)}) collective-permute-start(bf16[128,512]{1,0:T(8,128)(2,1)S(1)} %get-tuple-element.14), channel_id=1, source_target_pairs={{0,8},{8,16},{16,24},{1,9},{9,17},{17,25},{2,10},{10,18},{18,26},{... | collective-permute-start | bytes 393224 | tf_op jit(solution)/shard_map/ppermute | solution.py:22
  70.9 7.9 %collective-permute-start.5 = (bf16[128,512]{1,0:T(8,128)(2,1)S(1)}, bf16[128,512]{1,0:T(8,128)(2,1)S(1)}, u32[]{:S(2)}, u32[]{:S(2)}) collective-permute-start(bf16[128,512]{1,0:T(8,128)(2,1)S(1)} %get-tuple-element.15), channel_id=1, source_target_pairs={{8,0},{16,8},{24,16},{9,1},{17,9},{25,17},{10,2},{18,10},{26,18},{... | collective-permute-start | bytes 393224 | tf_op jit(solution)/shard_map/ppermute | solution.py:25
  78.8 7.2 %collective-permute-start.6 = (bf16[768,128]{1,0:T(8,128)(2,1)S(1)}, bf16[768,128]{1,0:T(8,128)(2,1)S(1)}, u32[]{:S(2)}, u32[]{:S(2)}) collective-permute-start(bf16[768,128]{1,0:T(8,128)(2,1)S(1)} %get-tuple-element.8), channel_id=1, source_target_pairs={{0,2},{2,4},{4,6},{1,3},{3,5},{5,7},{8,10},{10,12},{12,14},{9,11},... | collective-permute-start | bytes 589832 | tf_op jit(solution)/shard_map/ppermute | solution.py:22
  82.2 7.9 %collective-permute-start.7 = (bf16[768,128]{1,0:T(8,128)(2,1)S(1)}, bf16[768,128]{1,0:T(8,128)(2,1)S(1)}, u32[]{:S(2)}, u32[]{:S(2)}) collective-permute-start(bf16[768,128]{1,0:T(8,128)(2,1)S(1)} %get-tuple-element.9), channel_id=1, source_target_pairs={{2,0},{4,2},{6,4},{3,1},{5,3},{7,5},{10,8},{12,10},{14,12},{11,9},... | collective-permute-start | bytes 589832 | tf_op jit(solution)/shard_map/ppermute | solution.py:25
  90.2 0.7 copy-start.2
  91.2 4.6 %collective-permute-start.8 = (bf16[3,2,256]{2,0,1:T(4,128)(2,1)S(1)}, bf16[3,2,256]{2,0,1:T(4,128)(2,1)S(1)}, u32[]{:S(2)}, u32[]{:S(2)}) collective-permute-start(bf16[3,2,256]{2,0,1:T(4,128)(2,1)S(1)} %get-tuple-element.18), channel_id=1, source_target_pairs={{0,8},{8,16},{16,24},{1,9},{9,17},{17,25},{2,10},{10,18},{18,26},{... | collective-permute-start | bytes 9224 | tf_op jit(solution)/shard_map/ppermute | solution.py:22
  94.5 5.5 %collective-permute-start.9 = (bf16[3,2,256]{2,0,1:T(4,128)(2,1)S(1)}, bf16[3,2,256]{2,0,1:T(4,128)(2,1)S(1)}, u32[]{:S(2)}, u32[]{:S(2)}) collective-permute-start(bf16[3,2,256]{2,0,1:T(4,128)(2,1)S(1)} %get-tuple-element.19), channel_id=1, source_target_pairs={{8,0},{16,8},{24,16},{9,1},{17,9},{25,17},{10,2},{18,10},{26,18},{... | collective-permute-start | bytes 9224 | tf_op jit(solution)/shard_map/ppermute | solution.py:25
  100.2 5.9 %collective-permute-start.10 = (bf16[262,2,3]{2,0,1:T(8,128)(2,1)S(1)}, bf16[262,2,3]{2,0,1:T(8,128)(2,1)S(1)}, u32[]{:S(2)}, u32[]{:S(2)}) collective-permute-start(bf16[262,2,3]{2,0,1:T(8,128)(2,1)S(1)} %get-tuple-element.16), channel_id=1, source_target_pairs={{0,2},{2,4},{4,6},{1,3},{3,5},{5,7},{8,10},{10,12},{12,14},{9,11},... | collective-permute-start | bytes 9440 | tf_op jit(solution)/shard_map/ppermute | solution.py:22
  103.6 6.9 %collective-permute-start.11 = (bf16[262,2,3]{2,0,1:T(8,128)(2,1)S(1)}, bf16[262,2,3]{2,0,1:T(8,128)(2,1)S(1)}, u32[]{:S(2)}, u32[]{:S(2)}) collective-permute-start(bf16[262,2,3]{2,0,1:T(8,128)(2,1)S(1)} %get-tuple-element.17), channel_id=1, source_target_pairs={{2,0},{4,2},{6,4},{3,1},{5,3},{7,5},{10,8},{12,10},{14,12},{11,9},... | collective-permute-start | bytes 9440 | tf_op jit(solution)/shard_map/ppermute | solution.py:25
Sparse Core Ops, SparseCore 0:
  42.3 17.9 all-reduce.4
where the time goes:
time: 121 us; the launch traced here: 120 us
  waiting for transfers between devices  47.6 us (39%)
  starting transfers between devices  29.9 us (25%)
  matrix products  17.6 us (15%)
  between operations  15.2 us (13%)
  other arithmetic  7.13 us (6%)
  local copies, waits for them, and re-layouts  2.89 us (2%)
    ppermute x6, waiting for transfers between devices, with_halo(): lax.ppermute(lax.slice_in_dim(block, 0, width, axis=dim), axis, backward)  23.3 us
    ppermute x6, starting transfers between devices, with_halo(): lax.ppermute(lax.slice_in_dim(block, block.shape[dim] - width, None, axis...  22.1 us
    psum x1, waiting for transfers between devices, body(): lax.psum(grad_spec_im.astype(jnp.bfloat16), 'corner').astype(jnp.float32)  18.1 us
    dot_general x9, matrix products, matmul(): return jnp.dot(left, right, preferred_element_type=jnp.float32)  11.6 us
    ppermute x6, starting transfers between devices, with_halo(): lax.ppermute(lax.slice_in_dim(block, 0, width, axis=dim), axis, backward)  7.75 us
    ppermute x6, waiting for transfers between devices, with_halo(): lax.ppermute(lax.slice_in_dim(block, block.shape[dim] - width, None, axis...  6.14 us
    dot_general x16, matrix products, batched(): return jnp.einsum(form, left, right, preferred_element_type=jnp.float32)  5.61 us
    mul x3, other arithmetic, body(): advance(level_ext, speed_ext)  2.64 us
  transfers between devices with their start and end apart: 13, of which 11 were waited for; matrix products, arithmetic and copies ran while one was open for 3% of the time, Pallas kernels for 0%

commit v1 on v0

--- a/solution.py
+++ b/solution.py
@@ -166,7 +166,9 @@
     )
     grad_spec_re, grad_spec_im = (
         lax.psum(grad_spec_re.astype(jnp.bfloat16), "corner").astype(jnp.float32),
-        lax.psum(grad_spec_im.astype(jnp.bfloat16), "corner").astype(jnp.float32),
+        jnp.sum(lax.all_gather(grad_spec_im.astype(jnp.bfloat16), "corner"), axis=0).astype(
+            jnp.float32
+        ),
     )
     grad_window = window_grad(grad_spec_re, grad_spec_im, tables)
     framed_grad = with_halo(grad_window, (("ty", 0), ("tx", 1)), margin).astype(jnp.float32)

time: 121 us -> 93.2 us (0.77)
  waiting for transfers between devices: 47.6 us -> 29.1 us
  between operations: 15.2 us -> 1.77 us
  blocking collectives: 0 us -> 5.47 us
  matrix products: 17.6 us -> 15.3 us
    psum x1 -> x0, waiting for transfers between devices: 18.1 us -> none  [body(): lax.psum(grad_spec_im.astype(jnp.bfloat16), 'corner').astype(jnp.float32)]
    psum x0 -> x1, blocking collectives: none -> 3.59 us  [body(): lax.psum(grad_spec_re.astype(jnp.bfloat16), 'corner').astype(jnp.float32)]
    all_gather x0 -> x1, blocking collectives: none -> 1.88 us  [body(): lax.all_gather(grad_spec_im.astype(jnp.bfloat16), 'corner')]
    dot_general x9, matrix products: 11.6 us -> 9.94 us  [matmul(): return jnp.dot(left, right, preferred_element_type=jnp.float32)]
  transfers between devices with their start and end apart: 13 -> 12, of which waited for: 11 -> 10; matrix products, arithmetic and copies ran while one was open for 3% -> 3% of each run, Pallas kernels for 0% -> 0%
where the time goes in v1:
time: 93.2 us; the launch traced here: 92.6 us
  starting transfers between devices  30.8 us (33%)
  waiting for transfers between devices  29.1 us (31%)
  matrix products  15.3 us (16%)
  other arithmetic  7.3 us (8%)
  blocking collectives  5.47 us (6%)
  local copies, waits for them, and re-layouts  2.9 us (3%)
  between operations  1.77 us (2%)
    ppermute x6, starting transfers between devices, with_halo(): lax.ppermute(lax.slice_in_dim(block, block.shape[dim] - width, None, axis...  23.1 us
    ppermute x6, waiting for transfers between devices, with_halo(): lax.ppermute(lax.slice_in_dim(block, 0, width, axis=dim), axis, backward)  23 us
    dot_general x9, matrix products, matmul(): return jnp.dot(left, right, preferred_element_type=jnp.float32)  9.94 us
    ppermute x6, starting transfers between devices, with_halo(): lax.ppermute(lax.slice_in_dim(block, 0, width, axis=dim), axis, backward)  7.75 us
    ppermute x6, waiting for transfers between devices, with_halo(): lax.ppermute(lax.slice_in_dim(block, block.shape[dim] - width, None, axis...  6.16 us
    dot_general x16, matrix products, batched(): return jnp.einsum(form, left, right, preferred_element_type=jnp.float32)  5 us
    psum x1, blocking collectives, body(): lax.psum(grad_spec_re.astype(jnp.bfloat16), 'corner').astype(jnp.float32)  3.59 us
    mul x3, other arithmetic, body(): advance(level_ext, speed_ext)  2.64 us
  transfers between devices with their start and end apart: 12, of which 10 were waited for; matrix products, arithmetic and copies ran while one was open for 3% of the time, Pallas kernels for 0%

profile of v1, /device:TPU:0, one launch (start us, length us, event | category | flops | bytes accessed | tf_op | source)
XLA Modules:
  0.0 92.6 jit_solution(12575381115809106154)
XLA Ops:
  1.6 4.9 %collective-permute-start = (bf16[128,256]{1,0:T(8,128)(2,1)S(1)}, bf16[128,256]{1,0:T(8,128)(2,1)S(1)}, u32[]{:S(2)}, u32[]{:S(2)}) collective-permute-start(bf16[128,256]{1,0:T(8,128)(2,1)S(1)} %get-tuple-element.24), channel_id=1, source_target_pairs={{0,8},{8,16},{16,24},{1,9},{9,17},{17,25},{2,10},{10,18},{18,26},{... | collective-permute-start | bytes 196616 | tf_op jit(solution)/shard_map/ppermute | solution.py:22
  6.5 1.3 %collective-permute-start.1 = (bf16[128,256]{1,0:T(8,128)(2,1)S(1)}, bf16[128,256]{1,0:T(8,128)(2,1)S(1)}, u32[]{:S(2)}, u32[]{:S(2)}) collective-permute-start(bf16[128,256]{1,0:T(8,128)(2,1)S(1)} %get-tuple-element.25), channel_id=1, source_target_pairs={{8,0},{16,8},{24,16},{9,1},{17,9},{25,17},{10,2},{18,10},{26,18},{... | collective-permute-start | bytes 196616 | tf_op jit(solution)/shard_map/ppermute | solution.py:25
  9.0 1.1 %fusion.38 = (f32[128,512]{1,0:T(8,128)S(1)}, bf16[128,512]{1,0:T(8,128)(2,1)S(1)}, bf16[128,512]{1,0:T(8,128)(2,1)S(1)}) fusion(s32[128]{0:T(128)S(1)} %iota_add_fusion.1), kind=kLoop, calls=%fused_computation.78 | loop fusion | flops 1245184 | bytes 524800 | tf_op jit(solution)/shard_map/mul | solution.py:34
  11.1 1.6 %collective-permute-done.1 = bf16[128,256]{1,0:T(8,128)(2,1)S(1)} collective-permute-done((bf16[128,256]{1,0:T(8,128)(2,1)S(1)}, bf16[128,256]{1,0:T(8,128)(2,1)S(1)}, u32[]{:S(2)}, u32[]{:S(2)}) %collective-permute-start.1) | collective-permute-done | bytes 65568 | tf_op jit(solution)/shard_map/ppermute | solution.py:25
  12.7 3.5 %collective-permute-start.2 = (bf16[512,128]{1,0:T(8,128)(2,1)S(1)}, bf16[512,128]{1,0:T(8,128)(2,1)S(1)}, u32[]{:S(2)}, u32[]{:S(2)}) collective-permute-start(bf16[512,128]{1,0:T(8,128)(2,1)S(1)} %get-tuple-element.22), channel_id=1, source_target_pairs={{0,2},{2,4},{4,6},{1,3},{3,5},{5,7},{8,10},{10,12},{12,14},{9,11},... | collective-permute-start | bytes 393224 | tf_op jit(solution)/shard_map/ppermute | solution.py:22
  16.2 1.3 %collective-permute-start.3 = (bf16[512,128]{1,0:T(8,128)(2,1)S(1)}, bf16[512,128]{1,0:T(8,128)(2,1)S(1)}, u32[]{:S(2)}, u32[]{:S(2)}) collective-permute-start(bf16[512,128]{1,0:T(8,128)(2,1)S(1)} %get-tuple-element.23), channel_id=1, source_target_pairs={{2,0},{4,2},{6,4},{3,1},{5,3},{7,5},{10,8},{12,10},{14,12},{11,9},... | collective-permute-start | bytes 393224 | tf_op jit(solution)/shard_map/ppermute | solution.py:25
  18.7 4.4 %collective-permute-done.3 = bf16[512,128]{1,0:T(8,128)(2,1)S(1)} collective-permute-done((bf16[512,128]{1,0:T(8,128)(2,1)S(1)}, bf16[512,128]{1,0:T(8,128)(2,1)S(1)}, u32[]{:S(2)}, u32[]{:S(2)}) %collective-permute-start.3) | collective-permute-done | bytes 131104 | tf_op jit(solution)/shard_map/ppermute | solution.py:25
  23.4 1.2 %fusion.55 = f32[128,128]{1,0:T(8,128)S(1)} fusion(s32[128]{0:T(128)S(1)} %iota_add_fusion.1, bf16[256,512]{1,0:T(8,128)(2,1)S(1)} %convolution_convert_fusion.1), kind=kOutput, calls=%fused_computation.111 | convolution fusion | flops 17825792 | bytes 197120 | tf_op jit(solution)/shard_map/dot_general | solution.py:45
  24.6 1.2 %fusion.56 = f32[128,128]{1,0:T(8,128)S(1)} fusion(s32[128]{0:T(128)S(1)} %iota_add_fusion.1, bf16[256,512]{1,0:T(8,128)(2,1)S(1)} %convolution_convert_fusion.1), kind=kOutput, calls=%fused_computation.112 | convolution fusion | flops 17891328 | bytes 197120 | tf_op jit(solution)/shard_map/dot_general | solution.py:45
  25.8 1.2 %convolution_subtract_fusion.5 = f32[128,128]{1,0:T(8,128)S(1)} fusion(f32[128,128]{1,0:T(8,128)S(1)} %fusion.55, s32[128]{0:T(128)S(1)} %iota_add_fusion.1, bf16[256,512]{1,0:T(8,128)(2,1)S(1)} %convolution_convert_fusion.1), kind=kOutput, calls=%fused_computation.27 | convolution fusion | flops 17907712 | bytes 262656 | tf_op jit(solution)/shard_map/dot_general | solution.py:45
  27.1 1.2 %convolution_add_fusion.5 = f32[128,128]{1,0:T(8,128)S(1)} fusion(f32[128,128]{1,0:T(8,128)S(1)} %fusion.56, s32[128]{0:T(128)S(1)} %iota_add_fusion.1, bf16[256,512]{1,0:T(8,128)(2,1)S(1)} %convolution_convert_fusion.1), kind=kOutput, calls=%fused_computation.26 | convolution fusion | flops 17842176 | bytes 262656 | tf_op jit(solution)/shard_map/dot_general | solution.py:45
  35.0 3.6 %psum.7 = bf16[128,128]{0,1:T(8,128)(2,1)S(1)} all-reduce(bf16[128,128]{0,1:T(8,128)(2,1)S(1)} %get-tuple-element.2), channel_id=1, replica_groups=mesh['ty'=4,'tx'=4,'corner'=2] {'corner'}, use_global_device_ids=true, to_apply=%region_2.3 | all-reduce | flops 16384 | bytes 65536 | tf_op jit(solution)/shard_map/psum | solution.py:168
  38.6 1.2 %fusion.54 = f32[128,512]{1,0:T(8,128)S(1)} fusion(bf16[128,128]{0,1:T(8,128)(2,1)S(1)} %psum.7, s32[128]{0:T(128)S(1)} %iota_add_fusion.1), kind=kOutput, calls=%fused_computation.110 | convolution fusion | flops 17825792 | bytes 295424 | tf_op jit(solution)/shard_map/dot_general | solution.py:45
  39.8 1.9 %all-gather = bf16[256,128]{0,1:T(8,128)(2,1)S(1)} all-gather(bf16[128,128]{0,1:T(8,128)(2,1)S(1)} %get-tuple-element.3), channel_id=2, replica_groups=mesh['ty'=4,'tx'=4,'corner'=2] {'corner'}, dimensions={0}, use_global_device_ids=true | all-gather | bytes 98304 | tf_op jit(solution)/shard_map/all_gather | solution.py:169
  41.9 1.2 %fusion.53 = f32[128,512]{1,0:T(8,128)S(1)} fusion(bf16[128,128]{0,1:T(8,128)(2,1)S(1)} %reduce_sum.42, s32[128]{0:T(128)S(1)} %iota_add_fusion.1), kind=kOutput, calls=%fused_computation.109 | convolution fusion | flops 17825792 | bytes 295424 | tf_op jit(solution)/shard_map/dot_general | solution.py:45
  43.1 1.2 %fusion.8 = bf16[128,512]{1,0:T(8,128)(2,1)S(1)} fusion(f32[128,512]{1,0:T(8,128)S(1)} %fusion.54, bf16[128,128]{0,1:T(8,128)(2,1)S(1)} %reduce_sum.42, s32[128]{0:T(128)S(1)} %iota_add_fusion.1), kind=kOutput, calls=%fused_computation.24 | convolution fusion | flops 18022400 | bytes 426496 | tf_op jit(solution)/shard_map/dot_general | solution.py:45
  44.3 1.2 %fusion.9 = bf16[128,512]{1,0:T(8,128)(2,1)S(1)} fusion(f32[128,512]{1,0:T(8,128)S(1)} %fusion.53, bf16[128,128]{0,1:T(8,128)(2,1)S(1)} %psum.7, s32[128]{0:T(128)S(1)} %iota_add_fusion.1), kind=kOutput, calls=%fused_computation.25 | convolution fusion | flops 18022400 | bytes 426496 | tf_op jit(solution)/shard_map/dot_general | solution.py:45
  45.8 4.3 %collective-permute-start.4 = (bf16[128,512]{1,0:T(8,128)(2,1)S(1)}, bf16[128,512]{1,0:T(8,128)(2,1)S(1)}, u32[]{:S(2)}, u32[]{:S(2)}) collective-permute-start(bf16[128,512]{1,0:T(8,128)(2,1)S(1)} %get-tuple-element.12), channel_id=1, source_target_pairs={{0,8},{8,16},{16,24},{1,9},{9,17},{17,25},{2,10},{10,18},{18,26},{... | collective-permute-start | bytes 393224 | tf_op jit(solution)/shard_map/ppermute | solution.py:22
  50.1 1.3 %collective-permute-start.5 = (bf16[128,512]{1,0:T(8,128)(2,1)S(1)}, bf16[128,512]{1,0:T(8,128)(2,1)S(1)}, u32[]{:S(2)}, u32[]{:S(2)}) collective-permute-start(bf16[128,512]{1,0:T(8,128)(2,1)S(1)} %get-tuple-element.13), channel_id=1, source_target_pairs={{8,0},{16,8},{24,16},{9,1},{17,9},{25,17},{10,2},{18,10},{26,18},{... | collective-permute-start | bytes 393224 | tf_op jit(solution)/shard_map/ppermute | solution.py:25
  51.5 1.9 %collective-permute-done.4 = bf16[128,512]{1,0:T(8,128)(2,1)S(1)} collective-permute-done((bf16[128,512]{1,0:T(8,128)(2,1)S(1)}, bf16[128,512]{1,0:T(8,128)(2,1)S(1)}, u32[]{:S(2)}, u32[]{:S(2)}) %collective-permute-start.4) | collective-permute-done | bytes 131104 | tf_op jit(solution)/shard_map/ppermute | solution.py:22
  53.4 4.3 %collective-permute-done.5 = bf16[128,512]{1,0:T(8,128)(2,1)S(1)} collective-permute-done((bf16[128,512]{1,0:T(8,128)(2,1)S(1)}, bf16[128,512]{1,0:T(8,128)(2,1)S(1)}, u32[]{:S(2)}, u32[]{:S(2)}) %collective-permute-start.5) | collective-permute-done | bytes 131104 | tf_op jit(solution)/shard_map/ppermute | solution.py:25
  57.8 3.5 %collective-permute-start.6 = (bf16[768,128]{1,0:T(8,128)(2,1)S(1)}, bf16[768,128]{1,0:T(8,128)(2,1)S(1)}, u32[]{:S(2)}, u32[]{:S(2)}) collective-permute-start(bf16[768,128]{1,0:T(8,128)(2,1)S(1)} %get-tuple-element.6), channel_id=1, source_target_pairs={{0,2},{2,4},{4,6},{1,3},{3,5},{5,7},{8,10},{10,12},{12,14},{9,11},... | collective-permute-start | bytes 589832 | tf_op jit(solution)/shard_map/ppermute | solution.py:22
  61.3 1.3 %collective-permute-start.7 = (bf16[768,128]{1,0:T(8,128)(2,1)S(1)}, bf16[768,128]{1,0:T(8,128)(2,1)S(1)}, u32[]{:S(2)}, u32[]{:S(2)}) collective-permute-start(bf16[768,128]{1,0:T(8,128)(2,1)S(1)} %get-tuple-element.7), channel_id=1, source_target_pairs={{2,0},{4,2},{6,4},{3,1},{5,3},{7,5},{10,8},{12,10},{14,12},{11,9},... | collective-permute-start | bytes 589832 | tf_op jit(solution)/shard_map/ppermute | solution.py:25
  62.6 2.4 %collective-permute-done.6 = bf16[768,128]{1,0:T(8,128)(2,1)S(1)} collective-permute-done((bf16[768,128]{1,0:T(8,128)(2,1)S(1)}, bf16[768,128]{1,0:T(8,128)(2,1)S(1)}, u32[]{:S(2)}, u32[]{:S(2)}) %collective-permute-start.6) | collective-permute-done | bytes 196640 | tf_op jit(solution)/shard_map/ppermute | solution.py:22
  65.0 4.1 %collective-permute-done.7 = bf16[768,128]{1,0:T(8,128)(2,1)S(1)} collective-permute-done((bf16[768,128]{1,0:T(8,128)(2,1)S(1)}, bf16[768,128]{1,0:T(8,128)(2,1)S(1)}, u32[]{:S(2)}, u32[]{:S(2)}) %collective-permute-start.7) | collective-permute-done | bytes 196640 | tf_op jit(solution)/shard_map/ppermute | solution.py:25
  70.1 3.4 %collective-permute-start.8 = (bf16[3,2,256]{2,0,1:T(4,128)(2,1)S(1)}, bf16[3,2,256]{2,0,1:T(4,128)(2,1)S(1)}, u32[]{:S(2)}, u32[]{:S(2)}) collective-permute-start(bf16[3,2,256]{2,0,1:T(4,128)(2,1)S(1)} %get-tuple-element.16), channel_id=1, source_target_pairs={{0,8},{8,16},{16,24},{1,9},{9,17},{17,25},{2,10},{10,18},{18,26},{... | collective-permute-start | bytes 9224 | tf_op jit(solution)/shard_map/ppermute | solution.py:22
  73.5 1.3 %collective-permute-start.9 = (bf16[3,2,256]{2,0,1:T(4,128)(2,1)S(1)}, bf16[3,2,256]{2,0,1:T(4,128)(2,1)S(1)}, u32[]{:S(2)}, u32[]{:S(2)}) collective-permute-start(bf16[3,2,256]{2,0,1:T(4,128)(2,1)S(1)} %get-tuple-element.17), channel_id=1, source_target_pairs={{8,0},{16,8},{24,16},{9,1},{17,9},{25,17},{10,2},{18,10},{26,18},{... | collective-permute-start | bytes 9224 | tf_op jit(solution)/shard_map/ppermute | solution.py:25
  74.9 4.2 %collective-permute-done.9 = bf16[3,2,256]{2,0,1:T(4,128)(2,1)S(1)} collective-permute-done((bf16[3,2,256]{2,0,1:T(4,128)(2,1)S(1)}, bf16[3,2,256]{2,0,1:T(4,128)(2,1)S(1)}, u32[]{:S(2)}, u32[]{:S(2)}) %collective-permute-start.9) | collective-permute-done | bytes 3104 | tf_op jit(solution)/shard_map/ppermute | solution.py:25
  79.2 3.5 %collective-permute-start.10 = (bf16[262,2,3]{2,0,1:T(8,128)(2,1)S(1)}, bf16[262,2,3]{2,0,1:T(8,128)(2,1)S(1)}, u32[]{:S(2)}, u32[]{:S(2)}) collective-permute-start(bf16[262,2,3]{2,0,1:T(8,128)(2,1)S(1)} %get-tuple-element.14), channel_id=1, source_target_pairs={{0,2},{2,4},{4,6},{1,3},{3,5},{5,7},{8,10},{10,12},{12,14},{9,11},... | collective-permute-start | bytes 9440 | tf_op jit(solution)/shard_map/ppermute | solution.py:22
  82.7 1.3 %collective-permute-start.11 = (bf16[262,2,3]{2,0,1:T(8,128)(2,1)S(1)}, bf16[262,2,3]{2,0,1:T(8,128)(2,1)S(1)}, u32[]{:S(2)}, u32[]{:S(2)}) collective-permute-start(bf16[262,2,3]{2,0,1:T(8,128)(2,1)S(1)} %get-tuple-element.15), channel_id=1, source_target_pairs={{2,0},{4,2},{6,4},{3,1},{5,3},{7,5},{10,8},{12,10},{14,12},{11,9},... | collective-permute-start | bytes 9440 | tf_op jit(solution)/shard_map/ppermute | solution.py:25
  85.2 4.4 %collective-permute-done.11 = bf16[262,2,3]{2,0,1:T(8,128)(2,1)S(1)} collective-permute-done((bf16[262,2,3]{2,0,1:T(8,128)(2,1)S(1)}, bf16[262,2,3]{2,0,1:T(8,128)(2,1)S(1)}, u32[]{:S(2)}, u32[]{:S(2)}) %collective-permute-start.11) | collective-permute-done | bytes 3176 | tf_op jit(solution)/shard_map/ppermute | solution.py:25
  91.4 1.2 %slice_multiply_fusion.4 = f32[256,256]{1,0:T(8,128)} fusion(f32[262,262]{1,0:T(8,128)S(1)} %and_convert_fusion, f32[262,262]{1,0:T(8,128)S(1)} %get-tuple-element.5, f32[258,258]{1,0:T(8,128)S(1)} %slice_multiply_fusion), kind=kLoop, calls=%fused_computation.79 | loop fusion | flops 1245184 | bytes 2097152 | tf_op jit(solution)/shard_map/mul | solution.py:193
  (60 shorter events, 15.4 us)
Async XLA Ops:
  1.6 9.5 %collective-permute-start = (bf16[128,256]{1,0:T(8,128)(2,1)S(1)}, bf16[128,256]{1,0:T(8,128)(2,1)S(1)}, u32[]{:S(2)}, u32[]{:S(2)}) collective-permute-start(bf16[128,256]{1,0:T(8,128)(2,1)S(1)} %get-tuple-element.24), channel_id=1, source_target_pairs={{0,8},{8,16},{16,24},{1,9},{9,17},{17,25},{2,10},{10,18},{18,26},{... | collective-permute-start | bytes 196616 | tf_op jit(solution)/shard_map/ppermute | solution.py:22
  6.5 6.2 %collective-permute-start.1 = (bf16[128,256]{1,0:T(8,128)(2,1)S(1)}, bf16[128,256]{1,0:T(8,128)(2,1)S(1)}, u32[]{:S(2)}, u32[]{:S(2)}) collective-permute-start(bf16[128,256]{1,0:T(8,128)(2,1)S(1)} %get-tuple-element.25), channel_id=1, source_target_pairs={{8,0},{16,8},{24,16},{9,1},{17,9},{25,17},{10,2},{18,10},{26,18},{... | collective-permute-start | bytes 196616 | tf_op jit(solution)/shard_map/ppermute | solution.py:25
  12.7 6.0 %collective-permute-start.2 = (bf16[512,128]{1,0:T(8,128)(2,1)S(1)}, bf16[512,128]{1,0:T(8,128)(2,1)S(1)}, u32[]{:S(2)}, u32[]{:S(2)}) collective-permute-start(bf16[512,128]{1,0:T(8,128)(2,1)S(1)} %get-tuple-element.22), channel_id=1, source_target_pairs={{0,2},{2,4},{4,6},{1,3},{3,5},{5,7},{8,10},{10,12},{12,14},{9,11},... | collective-permute-start | bytes 393224 | tf_op jit(solution)/shard_map/ppermute | solution.py:22
  16.2 6.9 %collective-permute-start.3 = (bf16[512,128]{1,0:T(8,128)(2,1)S(1)}, bf16[512,128]{1,0:T(8,128)(2,1)S(1)}, u32[]{:S(2)}, u32[]{:S(2)}) collective-permute-start(bf16[512,128]{1,0:T(8,128)(2,1)S(1)} %get-tuple-element.23), channel_id=1, source_target_pairs={{2,0},{4,2},{6,4},{3,1},{5,3},{7,5},{10,8},{12,10},{14,12},{11,9},... | collective-permute-start | bytes 393224 | tf_op jit(solution)/shard_map/ppermute | solution.py:25
  30.6 1.0 %copy-start.1 = (s32[256,256]{1,0:T(8,128)S(1)}, s32[256,256]{1,0:T(8,128)}, u32[]{:S(2)}) copy-start(s32[256,256]{1,0:T(8,128)} %param.5) | copy-start | bytes 786436
  45.5 17.1 %copy-start = (s32[256,256]{1,0:T(8,128)S(1)}, s32[256,256]{1,0:T(8,128)}, u32[]{:S(2)}) copy-start(s32[256,256]{1,0:T(8,128)} %param.4) | copy-start | bytes 786436
  45.8 7.5 %collective-permute-start.4 = (bf16[128,512]{1,0:T(8,128)(2,1)S(1)}, bf16[128,512]{1,0:T(8,128)(2,1)S(1)}, u32[]{:S(2)}, u32[]{:S(2)}) collective-permute-start(bf16[128,512]{1,0:T(8,128)(2,1)S(1)} %get-tuple-element.12), channel_id=1, source_target_pairs={{0,8},{8,16},{16,24},{1,9},{9,17},{17,25},{2,10},{10,18},{18,26},{... | collective-permute-start | bytes 393224 | tf_op jit(solution)/shard_map/ppermute | solution.py:22
  50.1 7.6 %collective-permute-start.5 = (bf16[128,512]{1,0:T(8,128)(2,1)S(1)}, bf16[128,512]{1,0:T(8,128)(2,1)S(1)}, u32[]{:S(2)}, u32[]{:S(2)}) collective-permute-start(bf16[128,512]{1,0:T(8,128)(2,1)S(1)} %get-tuple-element.13), channel_id=1, source_target_pairs={{8,0},{16,8},{24,16},{9,1},{17,9},{25,17},{10,2},{18,10},{26,18},{... | collective-permute-start | bytes 393224 | tf_op jit(solution)/shard_map/ppermute | solution.py:25
  57.8 7.2 %collective-permute-start.6 = (bf16[768,128]{1,0:T(8,128)(2,1)S(1)}, bf16[768,128]{1,0:T(8,128)(2,1)S(1)}, u32[]{:S(2)}, u32[]{:S(2)}) collective-permute-start(bf16[768,128]{1,0:T(8,128)(2,1)S(1)} %get-tuple-element.6), channel_id=1, source_target_pairs={{0,2},{2,4},{4,6},{1,3},{3,5},{5,7},{8,10},{10,12},{12,14},{9,11},... | collective-permute-start | bytes 589832 | tf_op jit(solution)/shard_map/ppermute | solution.py:22
  61.3 7.9 %collective-permute-start.7 = (bf16[768,128]{1,0:T(8,128)(2,1)S(1)}, bf16[768,128]{1,0:T(8,128)(2,1)S(1)}, u32[]{:S(2)}, u32[]{:S(2)}) collective-permute-start(bf16[768,128]{1,0:T(8,128)(2,1)S(1)} %get-tuple-element.7), channel_id=1, source_target_pairs={{2,0},{4,2},{6,4},{3,1},{5,3},{7,5},{10,8},{12,10},{14,12},{11,9},... | collective-permute-start | bytes 589832 | tf_op jit(solution)/shard_map/ppermute | solution.py:25
  69.1 0.7 copy-start.2
  70.1 4.8 %collective-permute-start.8 = (bf16[3,2,256]{2,0,1:T(4,128)(2,1)S(1)}, bf16[3,2,256]{2,0,1:T(4,128)(2,1)S(1)}, u32[]{:S(2)}, u32[]{:S(2)}) collective-permute-start(bf16[3,2,256]{2,0,1:T(4,128)(2,1)S(1)} %get-tuple-element.16), channel_id=1, source_target_pairs={{0,8},{8,16},{16,24},{1,9},{9,17},{17,25},{2,10},{10,18},{18,26},{... | collective-permute-start | bytes 9224 | tf_op jit(solution)/shard_map/ppermute | solution.py:22
  73.5 5.5 %collective-permute-start.9 = (bf16[3,2,256]{2,0,1:T(4,128)(2,1)S(1)}, bf16[3,2,256]{2,0,1:T(4,128)(2,1)S(1)}, u32[]{:S(2)}, u32[]{:S(2)}) collective-permute-start(bf16[3,2,256]{2,0,1:T(4,128)(2,1)S(1)} %get-tuple-element.17), channel_id=1, source_target_pairs={{8,0},{16,8},{24,16},{9,1},{17,9},{25,17},{10,2},{18,10},{26,18},{... | collective-permute-start | bytes 9224 | tf_op jit(solution)/shard_map/ppermute | solution.py:25
  79.2 6.0 %collective-permute-start.10 = (bf16[262,2,3]{2,0,1:T(8,128)(2,1)S(1)}, bf16[262,2,3]{2,0,1:T(8,128)(2,1)S(1)}, u32[]{:S(2)}, u32[]{:S(2)}) collective-permute-start(bf16[262,2,3]{2,0,1:T(8,128)(2,1)S(1)} %get-tuple-element.14), channel_id=1, source_target_pairs={{0,2},{2,4},{4,6},{1,3},{3,5},{5,7},{8,10},{10,12},{12,14},{9,11},... | collective-permute-start | bytes 9440 | tf_op jit(solution)/shard_map/ppermute | solution.py:22
  82.7 6.9 %collective-permute-start.11 = (bf16[262,2,3]{2,0,1:T(8,128)(2,1)S(1)}, bf16[262,2,3]{2,0,1:T(8,128)(2,1)S(1)}, u32[]{:S(2)}, u32[]{:S(2)}) collective-permute-start(bf16[262,2,3]{2,0,1:T(8,128)(2,1)S(1)} %get-tuple-element.15), channel_id=1, source_target_pairs={{2,0},{4,2},{6,4},{3,1},{5,3},{7,5},{10,8},{12,10},{14,12},{11,9},... | collective-permute-start | bytes 9440 | tf_op jit(solution)/shard_map/ppermute | solution.py:25
